TPU v7x, 256 devices: a whole 4x4x8 slice. The times are simulated.
256 devices in a mesh: row: 16 (over y_lo, x, core), col: 16 (over z, y_hi).
Axes of the slice: x: 4, y: 4 (y_hi: 2, y_lo: 2; y = y_hi * 2 + y_lo), z: 8, core: 2. Of those that a mesh axis runs over, the one named last changes fastest.
Arguments:
- row_frames: float32 [3, 8192, 256], P(None, ('row', 'col')), may hold values from -40 to 40, as said below
- col_frames: float32 [3, 8192, 256], P(None, ('col', 'row')), may hold values from -40 to 40, as said below
- vectors: float32 [64, 8192], P(None, ('col', 'row')), may hold values from -6 to 6
Outputs:
- embedding_product: float32 [64, 8192], P(None, ('row', 'col'))
Inputs may be any that keep to these rules, and one draw needn't show every extreme that they name: `row_frames`: frames of one chain of 256 atoms, each rigidly rotated and moved and perturbed by its own amount. `col_frames`: frames of one chain of 256 atoms, each rigidly rotated and moved and perturbed by its own amount.
All inputs are finite; a program needn't handle non-finite values.
Results may differ from a plain program's by a relative error of at most 0.00017.
Values sent between devices are 32-bit elements; how exact they have to be, the bound alone decides.
A program may use at most 64 MiB of HBM per device.

v0:
```python
import jax
import jax.numpy as jnp
from jax import lax
from jax.sharding import PartitionSpec as P

NEWTON = 8
band_width = 2.0


def centre(frames):
    return frames - jnp.mean(frames, axis=2, keepdims=True)


def kernel_tile(rows, cols):
    count_rows = rows.shape[1]
    count_cols = cols.shape[1]
    atoms = rows.shape[2]
    row_norms = jnp.sum(rows * rows, axis=(0, 2))
    col_norms = jnp.sum(cols * cols, axis=(0, 2))
    product = jnp.dot(
        cols.reshape(3 * count_cols, atoms),
        rows.reshape(3 * count_rows, atoms).T,
        precision=lax.Precision.HIGHEST,
        preferred_element_type=jnp.float32,
    )
    product = product.reshape(3, count_cols, 3, count_rows)
    moment = [[product[second, :, first, :] for second in range(3)] for first in range(3)]
    half_norm = 0.5 * (row_norms[None, :] + col_norms[:, None])
    coef_two = -2.0 * sum(
        (moment[first][second] * moment[first][second] for first in range(3) for second in range(3))
    )
    coef_one = 8.0 * (
        moment[0][0] * moment[1][2] * moment[2][1]
        + moment[1][1] * moment[2][0] * moment[0][2]
        + moment[2][2] * moment[0][1] * moment[1][0]
    ) - 8.0 * (
        moment[0][0] * moment[1][1] * moment[2][2]
        + moment[1][2] * moment[2][0] * moment[0][1]
        + moment[2][1] * moment[1][0] * moment[0][2]
    )
    trace_one = moment[0][0] + moment[1][1] + moment[2][2]
    key_matrix = [
        [
            trace_one,
            moment[1][2] - moment[2][1],
            moment[2][0] - moment[0][2],
            moment[0][1] - moment[1][0],
        ],
        [
            moment[1][2] - moment[2][1],
            moment[0][0] - moment[1][1] - moment[2][2],
            moment[0][1] + moment[1][0],
            moment[2][0] + moment[0][2],
        ],
        [
            moment[2][0] - moment[0][2],
            moment[0][1] + moment[1][0],
            -moment[0][0] + moment[1][1] - moment[2][2],
            moment[1][2] + moment[2][1],
        ],
        [
            moment[0][1] - moment[1][0],
            moment[2][0] + moment[0][2],
            moment[1][2] + moment[2][1],
            -moment[0][0] - moment[1][1] + moment[2][2],
        ],
    ]
    minor_top = [
        key_matrix[0][0] * key_matrix[1][1] - key_matrix[1][0] * key_matrix[0][1],
        key_matrix[0][0] * key_matrix[1][2] - key_matrix[1][0] * key_matrix[0][2],
        key_matrix[0][0] * key_matrix[1][3] - key_matrix[1][0] * key_matrix[0][3],
        key_matrix[0][1] * key_matrix[1][2] - key_matrix[1][1] * key_matrix[0][2],
        key_matrix[0][1] * key_matrix[1][3] - key_matrix[1][1] * key_matrix[0][3],
        key_matrix[0][2] * key_matrix[1][3] - key_matrix[1][2] * key_matrix[0][3],
    ]
    minor_low = [
        key_matrix[2][0] * key_matrix[3][1] - key_matrix[3][0] * key_matrix[2][1],
        key_matrix[2][0] * key_matrix[3][2] - key_matrix[3][0] * key_matrix[2][2],
        key_matrix[2][0] * key_matrix[3][3] - key_matrix[3][0] * key_matrix[2][3],
        key_matrix[2][1] * key_matrix[3][2] - key_matrix[3][1] * key_matrix[2][2],
        key_matrix[2][1] * key_matrix[3][3] - key_matrix[3][1] * key_matrix[2][3],
        key_matrix[2][2] * key_matrix[3][3] - key_matrix[3][2] * key_matrix[2][3],
    ]
    coef_zero = (
        minor_top[0] * minor_low[5]
        - minor_top[1] * minor_low[4]
        + minor_top[2] * minor_low[3]
        + minor_top[3] * minor_low[2]
        - minor_top[4] * minor_low[1]
        + minor_top[5] * minor_low[0]
    )
    eigen = half_norm
    for newton_step in range(NEWTON):
        eigen_sq = eigen * eigen
        value = (eigen_sq + coef_two) * eigen_sq + coef_one * eigen + coef_zero
        slope = 4.0 * eigen_sq * eigen + 2.0 * coef_two * eigen + coef_one
        eigen = eigen - value / slope
    squared = jnp.maximum(2.0 * (half_norm - eigen) / atoms, 0.0)
    return jnp.exp(-squared / band_width)


def per_device(row_frames, col_frames, vectors):
    rows_own = centre(row_frames)
    cols_own = centre(col_frames)
    panel_rows = lax.all_gather(rows_own, "col", axis=1, tiled=True)
    tile = kernel_tile(panel_rows, lax.all_gather(cols_own, "row", axis=1, tiled=True))
    weighted = jnp.dot(
        lax.all_gather(vectors, "row", axis=1, tiled=True),
        tile,
        precision=lax.Precision.HIGHEST,
        preferred_element_type=jnp.float32,
    )
    degree = jnp.sum(tile, axis=0, keepdims=True)
    summed, total = (
        lax.psum_scatter(weighted, "col", scatter_dimension=1, tiled=True),
        lax.psum_scatter(degree, "col", scatter_dimension=1, tiled=True),
    )
    return summed / total


def solution(mesh):
    return jax.shard_map(
        per_device,
        mesh=mesh,
        in_specs=(
            P(None, ("row", "col"), None),
            P(None, ("col", "row"), None),
            P(None, ("col", "row")),
        ),
        out_specs=P(None, ("row", "col")),
        check_vma=False,
    )
```

profile of v0, /device:TPU:2, one launch (start us, length us, event | category | flops | bytes accessed | tf_op | source)
XLA Modules:
  0.0 559.0 jit_solution(16649390457122390750)
XLA Ops:
  6.5 1.0 reduce_sum.47
  7.5 1.6 broadcast_subtract_fusion
  9.1 0.0 all-gather.5.cloned.1.call-update
  9.2 0.0 all-gather.3.cloned.1.call-start
  9.2 1.0 reduce_sum.45
  10.2 1.6 broadcast_subtract_fusion.1
  11.8 0.0 all-gather.3.cloned.1.call-update
  11.8 0.0 reduce-scatter.9.cloned.1.call-start
  11.9 19.1 %all_gather.11 = f32[64,512]{0,1:T(8,128)S(1)} all-gather(f32[64,32]{0,1:T(8,128)} %param.5), channel_id=1, replica_groups=mesh['row'=16,'col'=16] {'row'}, dimensions={1}, use_global_device_ids=true | all-gather | bytes 139264 | tf_op jit(solution)/shard_map/all_gather | solution.py:108
  31.0 16.7 %all-gather.5.cloned.1.call-done = f32[3,512,256]{2,1,0:T(8,128)} async-done(((f32[3,32,256]{2,1,0:T(8,128)}), f32[3,512,256]{2,1,0:T(8,128)}) %all-gather.5.cloned.1.call-update) | async-done | bytes 1572880 | tf_op jit(solution)/shard_map/all_gather | solution.py:106
  47.7 1.7 multiply_reduce_fusion
  49.4 83.5 %all-gather.3.cloned.1.call-done = f32[3,512,256]{2,1,0:T(8,128)} async-done(((f32[3,32,256]{2,1,0:T(8,128)}), f32[3,512,256]{2,1,0:T(8,128)}) %all-gather.3.cloned.1.call-update) | async-done | bytes 1572880 | tf_op jit(solution)/shard_map/all_gather | solution.py:105
  132.9 9.8 %fusion = f32[3,512,3,512]{3,1,2,0:T(8,128)S(1)} fusion(f32[3,512,256]{2,1,0:T(8,128)S(1)} %copy-done, f32[3,512,256]{2,1,0:T(8,128)} %all-gather.3.cloned.1.call-done), kind=kOutput, calls=%fused_computation | convolution fusion | flops 7247757312 | bytes 12582912 | tf_op jit(solution)/shard_map/dot_general | solution.py:20
  142.7 0.2 multiply_reduce_fusion.1
  142.9 8.1 %fusion.42 = (f32[512]{0:T(512)S(1)}, f32[512,512]{1,0:T(8,128)S(1)}) fusion(f32[3,512,3,512]{3,1,2,0:T(8,128)S(1)} %fusion, f32[512]{0:T(512)S(1)} %multiply_reduce_fusion, f32[512]{0:T(512)S(1)} %multiply_reduce_fusion.1), kind=kLoop, calls=%fused_computation.77 | loop fusion | flops 52690432 | bytes 10491904 | tf_op jit(solution)/shard_map/reduce_sum | solution.py:113
  151.0 0.9 copy.10
  151.9 0.0 reduce-scatter.9.cloned.1.call-update
  151.9 0.0 reduce-scatter.7.cloned.1.call-start
  151.9 0.8 convolution_bitcast_fusion
  152.7 0.8 copy.8
  153.6 195.3 %reduce-scatter.9.cloned.1.call-done = f32[32,1]{1,0:T(8,128)} async-done(((f32[512,1]{1,0:T(8,128)}), f32[32,1]{1,0:T(8,128)}) %reduce-scatter.9.cloned.1.call-update) | async-done | bytes 144
  348.9 0.8 copy.11
  349.7 201.4 %reduce-scatter.7.cloned.1.call-done = f32[32,64]{1,0:T(8,128)} async-done(((f32[512,64]{1,0:T(8,128)}), f32[32,64]{1,0:T(8,128)}) %reduce-scatter.7.cloned.1.call-update) | async-done | bytes 8208
  551.0 1.4 bitcast_divide_fusion
  (8 shorter events, 0.0 us)
Async XLA Ops:
  6.5 41.1 %all-gather.5.cloned.1.call-start = ((), (), s32[]{:S(2)}) async-start(), calls=%async_computation.3 | async-start | bytes 1671168 | tf_op jit(solution)/shard_map/all_gather | solution.py:106
  9.2 123.7 %all-gather.3.cloned.1.call-start = ((), (), s32[]{:S(2)}) async-start(), calls=%async_computation.2 | async-start | bytes 1671168 | tf_op jit(solution)/shard_map/all_gather | solution.py:105
  11.8 337.0 %reduce-scatter.9.cloned.1.call-start = ((), (), s32[]{:S(2)}) async-start(), calls=%async_computation.5 | async-start | bytes 278528
  47.7 85.2 %copy-start = (f32[3,512,256]{2,1,0:T(8,128)S(1)}, f32[3,512,256]{2,1,0:T(8,128)}, u32[]{:S(2)}) copy-start(f32[3,512,256]{2,1,0:T(8,128)} %all-gather.5.cloned.1.call-done) | copy-start | bytes 4718596
  132.9 9.8 %copy-start.1 = (f32[3,512,256]{2,1,0:T(8,128)S(1)}, f32[3,512,256]{2,1,0:T(8,128)}, u32[]{:S(2)}) copy-start(f32[3,512,256]{2,1,0:T(8,128)} %all-gather.3.cloned.1.call-done) | copy-start | bytes 4718596
  151.9 399.1 %reduce-scatter.7.cloned.1.call-start = ((), (), s32[]{:S(2)}) async-start(), calls=%async_computation.4 | async-start | bytes 278528
Sparse Core Ops, SparseCore 0:
  9.3 38.3 all-gather.4
  50.3 82.5 all-gather.2
  152.0 196.8 reduce-scatter.8
  353.0 198.0 reduce-scatter.6
where the time goes:
time: 559 us
  waiting for transfers between devices  497 us (89%)
  blocking collectives  19.1 us (3%)
  other arithmetic  16.6 us (3%)
  between operations  13.2 us (2%)
  matrix products  10.6 us (2%)
    unnamed x6, waiting for transfers between devices  397 us
    all_gather x1, waiting for transfers between devices, per_device(): panel_rows = lax.all_gather(rows_own, 'col', axis=1, tiled=True)  83.5 us
    all_gather x1, blocking collectives, per_device(): lax.all_gather(vectors, 'row', axis=1, tiled=True)  19.1 us
    all_gather x1, waiting for transfers between devices, per_device(): lax.all_gather(cols_own, 'row', axis=1, tiled=True)  16.7 us
  transfers between devices with their start and end apart: 4, of which 4 were waited for; matrix products, arithmetic and copies ran while one was open for 1% of the time, Pallas kernels for 0%

commit v1 on v0

--- a/solution.py
+++ b/solution.py
@@ -103,7 +103,12 @@
     rows_own = centre(row_frames)
     cols_own = centre(col_frames)
     panel_rows = lax.all_gather(rows_own, "col", axis=1, tiled=True)
-    tile = kernel_tile(panel_rows, lax.all_gather(cols_own, "row", axis=1, tiled=True))
+    tile = kernel_tile(
+        panel_rows,
+        jnp.concatenate(
+            lax.all_to_all(jnp.stack([cols_own] * lax.axis_size("row")), "row", 0, 0), axis=1
+        ),
+    )
     weighted = jnp.dot(
         lax.all_gather(vectors, "row", axis=1, tiled=True),
         tile,

time: 559 us -> 527 us (0.943)
  waiting for transfers between devices: 497 us -> 445 us
  blocking collectives: 19.1 us -> 32.6 us
  starting transfers between devices: 0.13 us -> 6.07 us
    all_gather x1, waiting for transfers between devices: 83.5 us -> 48.9 us  [per_device(): panel_rows = lax.all_gather(rows_own, 'col', axis=1, tiled=True)]
    all_gather x1 -> x0, waiting for transfers between devices: 16.7 us -> none  [per_device(): lax.all_gather(cols_own, 'row', axis=1, tiled=True)]
    all_gather x1, blocking collectives: 19.1 us -> 32.6 us  [per_device(): lax.all_gather(vectors, 'row', axis=1, tiled=True)]
    all_to_all x0 -> x1, starting transfers between devices: none -> 5.99 us  [per_device(): lax.all_to_all(jnp.stack([cols_own] * lax.axis_size('row')), 'row', 0, 0)]
    unnamed x6 -> x5, waiting for transfers between devices: 397 us -> 397 us
  transfers between devices with their start and end apart: 4 -> 4, of which waited for: 4 -> 3; matrix products, arithmetic and copies ran while one was open for 1% -> 1% of each run, Pallas kernels for 0% -> 0%
where the time goes in v1:
time: 527 us
  waiting for transfers between devices  445 us (84%)
  blocking collectives  32.6 us (6%)
  other arithmetic  16 us (3%)
  between operations  13.2 us (3%)
  matrix products  9.04 us (2%)
  starting transfers between devices  6.07 us (1%)
    unnamed x5, waiting for transfers between devices  397 us
    all_gather x1, waiting for transfers between devices, per_device(): panel_rows = lax.all_gather(rows_own, 'col', axis=1, tiled=True)  48.9 us
    all_gather x1, blocking collectives, per_device(): lax.all_gather(vectors, 'row', axis=1, tiled=True)  32.6 us
  transfers between devices with their start and end apart: 4, of which 3 were waited for; matrix products, arithmetic and copies ran while one was open for 1% of the time, Pallas kernels for 0%

profile of v1, /device:TPU:2, one launch (start us, length us, event | category | flops | bytes accessed | tf_op | source)
XLA Modules:
  0.0 526.6 jit_solution(10172562669899155118)
XLA Ops:
  6.5 1.0 reduce_sum.45
  7.5 1.6 broadcast_subtract_fusion.1
  9.2 1.0 reduce_sum.47
  10.2 1.0 broadcast_subtract_fusion
  11.1 1.3 stack.2
  12.5 6.0 %all-to-all-start = ((f32[16,3,32,256]{3,2,1,0:T(8,128)}), f32[16,3,32,256]{3,2,1,0:T(8,128)S(1)}, u32[]{:S(2)}, u32[]{:S(2)}) async-start(f32[16,3,32,256]{3,2,1,0:T(8,128)} %stack.2), calls=%async_computation | async-start | bytes 3145728 | tf_op jit(solution)/shard_map/all_to_all | solution.py:109
  18.5 0.0 reduce-scatter.9.cloned.1.call-start
  18.5 32.6 %all_gather.7 = f32[64,512]{0,1:T(8,128)S(1)} all-gather(f32[64,32]{0,1:T(8,128)S(1)} %copy-done.1), channel_id=1, replica_groups=mesh['row'=16,'col'=16] {'row'}, dimensions={1}, use_global_device_ids=true | all-gather | bytes 139264 | tf_op jit(solution)/shard_map/all_gather | solution.py:113
  51.1 0.2 multiply_reduce_fusion
  51.3 0.1 add.209
  51.4 0.2 copy.7
  51.6 48.9 %all-gather.2.cloned.1.call-done = f32[3,512,256]{2,1,0:T(8,128)} async-done(((f32[3,32,256]{2,1,0:T(8,128)}), f32[3,512,256]{2,1,0:T(8,128)}) %all-gather.2.cloned.1.call-update) | async-done | bytes 1572880 | tf_op jit(solution)/shard_map/all_gather | solution.py:105
  100.5 1.7 multiply_reduce_fusion.1
  102.2 0.2 copy-done
  102.4 8.3 %fusion = f32[3,512,3,512]{3,1,2,0:T(8,128)S(1)} fusion(f32[3,512,256,1]{2,1,3,0:T(8,128)S(1)} %bitcast.86, f32[3,512,256]{2,1,0:T(8,128)S(1)} %copy-done), kind=kOutput, calls=%fused_computation | convolution fusion | flops 7247757312 | bytes 12582912 | tf_op jit(solution)/shard_map/dot_general | solution.py:20
  110.6 8.1 %fusion.41 = (f32[512]{0:T(512)S(1)}, f32[512,512]{1,0:T(8,128)S(1)}) fusion(f32[3,512,3,512]{3,1,2,0:T(8,128)S(1)} %fusion, f32[512]{0:T(512)S(1)} %add.209, f32[512]{0:T(512)S(1)} %multiply_reduce_fusion.1), kind=kLoop, calls=%fused_computation.76 | loop fusion | flops 52690432 | bytes 10491904 | tf_op jit(solution)/shard_map/reduce_sum | solution.py:118
  118.8 0.9 copy.12
  119.6 0.0 reduce-scatter.7.cloned.1.call-start
  119.7 0.8 convolution_bitcast_fusion
  120.5 0.8 copy.10
  121.3 195.1 %reduce-scatter.9.cloned.1.call-done = f32[32,1]{1,0:T(8,128)} async-done(((f32[512,1]{1,0:T(8,128)}), f32[32,1]{1,0:T(8,128)}) %reduce-scatter.9.cloned.1.call-update) | async-done | bytes 144
  316.4 0.8 copy.13
  317.2 201.4 %reduce-scatter.7.cloned.1.call-done = f32[32,64]{1,0:T(8,128)} async-done(((f32[512,64]{1,0:T(8,128)}), f32[32,64]{1,0:T(8,128)}) %reduce-scatter.7.cloned.1.call-update) | async-done | bytes 8208
  518.6 1.4 bitcast_divide_fusion
  (10 shorter events, 0.1 us)
Async XLA Ops:
  6.5 93.9 %all-gather.2.cloned.1.call-start = ((), (), s32[]{:S(2)}) async-start(), calls=%async_computation.3 | async-start | bytes 1671168 | tf_op jit(solution)/shard_map/all_gather | solution.py:105
  12.5 6.0 %copy-start.1 = (f32[64,32]{0,1:T(8,128)S(1)}, f32[64,32]{0,1:T(8,128)}, u32[]{:S(2)}) copy-start(f32[64,32]{0,1:T(8,128)} %param.5) | copy-start | bytes 24580
  12.5 38.7 %all-to-all-start = ((f32[16,3,32,256]{3,2,1,0:T(8,128)}), f32[16,3,32,256]{3,2,1,0:T(8,128)S(1)}, u32[]{:S(2)}, u32[]{:S(2)}) async-start(f32[16,3,32,256]{3,2,1,0:T(8,128)} %stack.2), calls=%async_computation | async-start | bytes 3145728 | tf_op jit(solution)/shard_map/all_to_all | solution.py:109
  18.5 298.0 %reduce-scatter.9.cloned.1.call-start = ((), (), s32[]{:S(2)}) async-start(), calls=%async_computation.5 | async-start | bytes 278528
  100.5 1.9 copy-start
  119.6 399.0 %reduce-scatter.7.cloned.1.call-start = ((), (), s32[]{:S(2)}) async-start(), calls=%async_computation.4 | async-start | bytes 278528
Sparse Core Ops, SparseCore 0:
  10.0 90.4 all-gather.1
  119.8 196.6 reduce-scatter.8
  320.7 197.8 reduce-scatter.6
